TPU v7x, 32 devices: a whole 2x2x4 slice. The times are simulated.
32 devices in a mesh: gx: 4 (over y, x), gy: 4 (over z), ga: 2 (over core).
Axes of the slice: x: 2, y: 2, z: 4, core: 2. Of those that a mesh axis runs over, the one named last changes fastest.
Arguments:
- fields: float32 [5, 16, 64, 1024], P(None, 'ga', 'gx', 'gy'), may hold values from -6 to 6
- stiffness: float32 [16, 64, 1024], P('ga', 'gx', 'gy'), may hold values from 0.25 to 4
- lift_weight: float32 [5, 32], replicated, may hold values from -2.5 to 2.5
- lift_bias: float32 [32], replicated, may hold values from -3 to 3
- mix_weight: bfloat16 [32, 32], replicated, may hold values from -0.5 to 0.5
- spectral_weight: float32 [8, 32, 32, 32, 128], P('ga', 'gy', None, 'gx'), may hold values from -0.48 to 0.48
- output_bias: float32 [32], replicated, may hold values from -3 to 3
Outputs:
- layer_out: bfloat16 [16, 32, 32, 512], P('ga', None, 'gx', 'gy')
All inputs are finite; a program needn't handle non-finite values.
Results may differ from a plain program's by a relative error of at most 0.01.
Values may be sent and summed in bfloat16 or wider, within the bound.
A program may use at most 128 MiB of HBM per device.

v0:
```python
import math

import contextlib
import functools
import jax
import jax.numpy as jnp
import numpy as np
from jax import lax
from jax.experimental import pallas as pl
from jax.experimental.pallas import tpu as pltpu
from jax.sharding import PartitionSpec as P

STEPS = 3
MX = 32
MY = 64
MZ = 8
DEPTH_CHUNKS = 4
LIFT_CHUNKS = 4


courant_half = 0.1
smooth_half = 0.15
mean_flow = (0.3, -0.2, 0.1)
highest = lax.Precision.HIGHEST


MESH = pl.DeviceIdType.MESH
f32 = jnp.float32
bf16 = jnp.bfloat16


def gelu(v):
    return 0.5 * v * (1.0 + jnp.tanh(math.sqrt(2.0 / math.pi) * (v + 0.044715 * (v * v * v))))


def mark(name):
    return contextlib.nullcontext()


def swapped(v):
    sign = jnp.where(lax.broadcasted_iota(jnp.int32, v.shape, 1) < MY, 1.0, -1.0)
    return pltpu.roll(v, MY, 1) * sign


def dot(a, b, dims=((1,), (0,))):
    return lax.dot_general(a, b, (dims, ((), ())), preferred_element_type=f32)


def peers(axis):
    count = lax.axis_size(axis)
    me = lax.axis_index(axis)
    return me, [(d, lax.rem(me + d, count), lax.rem(me + count - d, count)) for d in range(1, count)]


def remote(src, dst, send, recv, axis, peer):
    return pltpu.make_async_remote_copy(
        src_ref=src,
        dst_ref=dst,
        send_sem=send,
        recv_sem=recv,
        device_id={axis: peer},
        device_id_type=MESH,
    )


def stencil_step(state, target, stiff, xr, yr, dims):
    NZ, NX, NY = dims
    eye = lax.broadcasted_iota(jnp.int32, (NZ * NX, NZ * NX), 0) == lax.broadcasted_iota(
        jnp.int32, (NZ * NX, NZ * NX), 1
    )
    columns = [
        [
            jnp.sum(
                jnp.where(eye, jnp.broadcast_to(yr[side, f : f + 1, :], eye.shape), 0.0),
                axis=1,
                keepdims=True,
            )
            for f in range(5)
        ]
        for side in range(2)
    ]
    row = lax.broadcasted_iota(jnp.int32, (NX, NY), 0)
    lane = lax.broadcasted_iota(jnp.int32, (NX, NY), 1)
    a, b = courant_half, smooth_half
    for z in range(NZ):
        near = []
        for f in range(5):
            c = state[f, z + 1]
            span = slice(z * NX, (z + 1) * NX)
            xl = jnp.where(row == 0, xr[0, f, z : z + 1, :].astype(f32), pltpu.roll(c, 1, 0))
            xu = jnp.where(row == NX - 1, xr[1, f, z : z + 1, :].astype(f32), pltpu.roll(c, NX - 1, 0))
            yl = jnp.where(lane == 0, columns[0][f][span], pltpu.roll(c, 1, 1))
            yu = jnp.where(lane == NY - 1, columns[1][f][span], pltpu.roll(c, NY - 1, 1))
            near.append((c, xl, xu, yl, yu, state[f, z], state[f, z + 2]))
        diverge = (
            (near[1][2] - near[1][1]) + (near[2][4] - near[2][3]) + (near[3][6] - near[3][5])
        )
        p = near[4]
        coupling = (diverge, p[2] - p[1], p[4] - p[3], p[6] - p[5], stiff[z] * diverge)
        for f in range(5):
            c, xl, xu, yl, yu, zl, zu = near[f]
            target[f, z + 1] = (
                (1.0 - 6.0 * b) * c
                + (b + a * mean_flow[0]) * xl
                + (b - a * mean_flow[0]) * xu
                + (b + a * mean_flow[1]) * yl
                + (b - a * mean_flow[1]) * yu
                + (b + a * mean_flow[2]) * zl
                + (b - a * mean_flow[2]) * zu
                - a * coupling[f]
            )


def layer_kernel(
    cfg,
    fields_hbm, stiff_hbm, ed_hbm, et_hbm, x1_hbm, x2_hbm, w_hbm, lw_hbm, lb_hbm, mix_hbm, bias_hbm,
    out,
    state, stiff, xs, xr, ys, yr, pairs, filt, ed, et, x1, x2, wv, lw, lb, mix, bias_row, wide_lift,
    lift, lift_in, both, tf, tb, p2, r2, q3, r3, c4, r4, rr, ii, mf, r5, b6, r6, r7, acc,
    local, sent, hr, r1s, r2s, r3s, r4s, r5s, r6s, r7s,
):
    G, H, A, C, CB, KB, OB, KZ, NZL, XL, YL = cfg
    Q = 2 * MY
    NX, NY = 2 * XL, 2 * YL
    gx, gx_peers = peers("gx")
    gy, gy_peers = peers("gy")
    ga = lax.axis_index("ga")
    other = lax.rem(ga + 1, A)
    barrier = pltpu.get_barrier_semaphore()
    for axis, group in (("gx", gx_peers), ("gy", gy_peers)):
        for _, peer, _ in group:
            pl.semaphore_signal(barrier, inc=1, device_id={axis: peer}, device_id_type=MESH)
    pl.semaphore_signal(barrier, inc=1, device_id={"ga": other}, device_id_type=MESH)
    loads = [
        pltpu.make_async_copy(source, target, local.at[n])
        for n, (source, target) in enumerate(
            (
                (fields_hbm, state.at[0, :, pl.ds(1, NZL)]),
                (stiff_hbm, stiff),
                (ed_hbm.at[gy], ed),
                (et_hbm.at[gy], et),
                (x1_hbm, x1),
                (x2_hbm, x2),
                (w_hbm, wv),
                (lw_hbm, lw),
                (lb_hbm, lb),
                (mix_hbm, mix),
                (bias_hbm, bias_row),
            )
        )
    ]
    loads[0].start()

    HALF = KZ // 2
    NZC = DEPTH_CHUNKS
    ZC = NZL // NZC
    NZ = NZL * A
    slots = list(range(0, KZ, 2)) + list(range(1, KZ, 2))

    def own(values):
        picked = jnp.float32(values[0])
        for n in range(1, A):
            picked = jnp.where(ga == n, jnp.float32(values[n]), picked)
        return picked

    def angles(z, owner, k):
        v = [
            2.0 * math.pi * ((((n + owner) % A * KZ + k) * (n * NZL + z)) % NZ) / NZ for n in range(A)
        ]
        return own([math.cos(x) for x in v]), own([math.sin(x) for x in v])

    def build_table():
        loads[2].wait()
        loads[3].wait()
        for z in range(NZL):
            for owner in range(A):
                for j, k in enumerate(slots):
                    cos, sin = angles(z, owner, k)
                    span = slice((j % HALF) * Q, (j % HALF + 1) * Q)
                    if owner == 0:
                        block = ed[0] * cos + ed[1] * sin
                        tf[j // HALF, z * YL : (z + 1) * YL, span] = block.astype(bf16)
                    block = et[0] * cos + et[1] * sin
                    tb[2 * owner + j // HALF, span, z * YL : (z + 1) * YL] = block.astype(bf16)

    spread = jnp.where(
        lax.broadcasted_iota(jnp.int32, (C * XL, C), 0) // XL
        == lax.broadcasted_iota(jnp.int32, (C * XL, C), 1),
        1.0,
        0.0,
    )

    def tall(values):
        return jnp.sum(spread * values, axis=1, keepdims=True)

    def build_lift():
        for n in (7, 8):
            loads[n].wait()
        for f in range(6):
            values = lw[f : f + 1, :] if f < 5 else lb[...]
            wide_lift[f] = jnp.broadcast_to(tall(values), (C * XL, YL))

    with mark("ld0"):
        loads[0].wait()
    eye = lax.broadcasted_iota(jnp.int32, (NZL * NX, NZL * NX), 0) == lax.broadcasted_iota(
        jnp.int32, (NZL * NX, NZL * NX), 1
    )
    for t in range(STEPS):
        now = state.at[t]
        with mark("pack%d" % t):
            for side, (edge_x, edge_y) in enumerate(((NX - 1, NY - 1), (0, 0))):
                for f in range(5):
                    for z in range(NZL):
                        row = now[f, z + 1, edge_x : edge_x + 1, :]
                        xs[t, side, f, z : z + 1, :] = row.astype(bf16)
                    column = now[f, 1 : NZL + 1, :, edge_y : edge_y + 1].reshape(NZL * NX, 1)
                    ys[t, side, f : f + 1, :] = jnp.sum(
                        jnp.where(eye, jnp.broadcast_to(column, eye.shape), 0.0),
                        axis=0,
                        keepdims=True,
                    )
        if t == 0:
            with mark("barrier"):
                pl.semaphore_wait(barrier, (G - 1) + (H - 1) + 1)
        for side in range(2):
            shift = 1 if side == 0 else -1
            tx, ty, ta = (
                lax.rem(lax.axis_index(n) + lax.axis_size(n) + shift, lax.axis_size(n))
                for n in ("gx", "gy", "ga")
            )
            plane, halo = (NZL, 0) if side == 0 else (1, NZL + 1)
            remote(ys.at[t, side], yr.at[t, side], sent.at[0], hr.at[t, 0], "gy", ty).start()
            remote(xs.at[t, side], xr.at[t, side], sent.at[1], hr.at[t, 1], "gx", tx).start()
            remote(now.at[:, plane], now.at[:, halo], sent.at[2], hr.at[t, 2], "ga", ta).start()
        if t == 0:
            for load in loads[1:]:
                load.start()
            with mark("table"):
                build_table()
                loads[1].wait()
        if t == STEPS - 1:
            with mark("buildlift"):
                build_lift()
        with mark("halo%d" % t):
            remote(ys.at[t], yr.at[t], sent.at[0], hr.at[t, 0], "gy", gy).wait_recv()
            remote(xs.at[t], xr.at[t], sent.at[1], hr.at[t, 1], "gx", gx).wait_recv()
            two = now.at[:, pl.ds(0, 2)]
            remote(two, two, sent.at[2], hr.at[t, 2], "ga", other).wait_recv()
        with mark("stencil%d" % t):
            stencil_step(now, state.at[t + 1], stiff, xr.at[t], yr.at[t], (NZL, NX, NY))

    with mark("filter"):
        twin = lax.broadcasted_iota(jnp.int32, (NY, YL), 0) // 2 == lax.broadcasted_iota(
            jnp.int32, (NY, YL), 1
        )
        twin = jnp.where(twin, 1.0, 0.0)
        for f in range(5):
            pairs[f] = lax.dot_general(
                state[STEPS, f, 1 : NZL + 1].reshape(NZL * NX, NY),
                twin,
                (((1,), (0,)), ((), ())),
                precision=highest,
                preferred_element_type=f32,
            )
            for z in range(NZL):
                filt[f, z] = 0.25 * (
                    pairs[f, pl.ds(z * NX, XL, stride=2), :]
                    + pairs[f, pl.ds(z * NX + 1, XL, stride=2), :]
                )

    def lift_two(pair, carry):
        rows = pl.ds(pl.multiple_of(pair * 2 * XL, 2 * XL), 2 * XL)
        weights = [wide_lift[f, rows, :] for f in range(6)]
        for z in range(NZL):
            v = weights[5]
            for f in range(5):
                v = v + jnp.concatenate([filt[f, z], filt[f, z]], axis=0) * weights[f]
            lift[rows, z * YL : (z + 1) * YL] = gelu(v).astype(bf16)
        return carry

    LC = LIFT_CHUNKS
    RC = C * XL // LC
    with mark("lift"):
        for n in range(LC):
            lax.fori_loop(n * C // 2 // LC, (n + 1) * C // 2 // LC, lift_two, 0)
            rows = pl.ds(n * RC, RC)
            remote(lift.at[rows], lift_in.at[rows], sent.at[3], r1s.at[n], "ga", other).start()
    for n in range(LC):
        rows = pl.ds(n * RC, RC)
        with mark("w1"):
            remote(lift.at[rows], lift_in.at[rows], sent.at[3], r1s.at[n], "ga", other).wait_recv()
        with mark("sumdiff"):
            mine, theirs = lift[rows], lift_in[rows]
            both[0, rows] = mine + theirs
            both[1, rows] = mine - theirs

    for parity in range(2):
        with mark("dot1"):
            modes = dot(both[parity], tf[parity]).astype(bf16)
            for i in range(HALF):
                h = parity * HALF + i
                p2[h] = modes[:, i * Q : (i + 1) * Q].reshape(p2.shape[1:])
        for i in range(HALF):
            h = parity * HALF + i
            for _, peer, _ in gx_peers:
                remote(p2.at[h, peer], r2.at[h, gx], sent.at[4], r2s.at[h], "gx", peer).start()
            r2[h, gx] = p2[h, gx]

    with mark("direct"):
        loads[9].wait()
        loads[10].wait()
        bias = tall(bias_row[...])
        wide = dot(spread.astype(bf16), mix[...], ((1,), (1,))).astype(bf16)
        wide = dot(wide, spread.astype(bf16), ((1,), (1,)))
        same = lax.rem(lax.broadcasted_iota(jnp.int32, wide.shape, 0), XL) == lax.rem(
            lax.broadcasted_iota(jnp.int32, wide.shape, 1), XL
        )
        mixk = jnp.where(same, wide, 0.0).astype(bf16)
        for j in range(NZC):
            span = slice(j * ZC * YL, (j + 1) * ZC * YL)
            acc[:, span] = dot(mixk, lift[:, span]) + bias
        loads[4].wait()
        loads[5].wait()
        loads[6].wait()

    def turn(x, v):
        both_parts = dot(x[...], v)
        rows = both_parts.shape[0] // 2
        return (both_parts[:rows] + swapped(both_parts[rows:])).astype(bf16)

    def step_x(h):
        part = r2.at[h, pl.ds(0, G - 1)]
        with mark("w2"):
            remote(part, part, sent.at[4], r2s.at[h], "gx", gx).wait_recv()
        with mark("xdot"):
            q3[h] = turn(x1, r2[h].reshape(C * XL, Q)).reshape(q3.shape[1:])
        for n, peer, _ in gy_peers:
            remote(q3.at[h, peer], r3.at[h, n - 1], sent.at[5], r3s.at[h], "gy", peer).start()

    def step_y(h):
        with mark("w3"):
            remote(r3.at[h], r3.at[h], sent.at[5], r3s.at[h], "gy", gy).wait_recv()
        total = q3[h, gy].astype(f32)
        for n in range(H - 1):
            total = total + r3[h, n].astype(f32)
        c4[h] = total.astype(bf16)
        for _, peer, _ in gx_peers:
            remote(c4.at[h], r4.at[h, gx], sent.at[6], r4s.at[h], "gx", peer).start()
        r4[h, gx] = c4[h]

    low = lax.broadcasted_iota(jnp.int32, (C * KB, Q), 1) < MY

    def step_mix(h):
        part = r4.at[h, pl.ds(0, G - 1)]
        with mark("w4"):
            remote(part, part, sent.at[6], r4s.at[h], "gx", gx).wait_recv()
        with mark("mix"):
            v = r4[h].reshape(C * KB, Q).astype(f32)
            turned = pltpu.roll(v, MY, 1)
            rr[h] = jnp.where(low, v, turned)
            ii[h] = jnp.where(low, turned, v)

            def mix_one(kx, carry):
                a = [None] * 4
                b = [None] * 4
                for c in range(C):
                    w = wv[slots[h], kx, c]
                    x = w * rr[h, pl.ds(c * KB + kx, 1), :]
                    y = w * ii[h, pl.ds(c * KB + kx, 1), :]
                    n = c % 4
                    a[n] = x if a[n] is None else a[n] + x
                    b[n] = y if b[n] is None else b[n] + y
                mf[h, kx] = ((a[0] + a[1]) + (a[2] + a[3])) - swapped((b[0] + b[1]) + (b[2] + b[3]))
                return carry

            lax.fori_loop(0, KB, mix_one, 0)
            r5[h, gy] = mf[h].reshape(KB * OB, Q).astype(bf16)
        for _, peer, _ in gy_peers:
            remote(r5.at[h, gy], r5.at[h, gy], sent.at[7], r5s.at[h], "gy", peer).start()

    def step_back(h):
        part = r5.at[h, pl.ds(0, H - 1)]
        with mark("w5"):
            remote(part, part, sent.at[7], r5s.at[h], "gy", gy).wait_recv()
        with mark("back"):
            b6[h] = turn(x2, r5[h].reshape(H * KB * OB, Q)).reshape(b6.shape[1:])
        for _, peer, _ in gx_peers:
            remote(b6.at[h, peer], r6.at[h, gx], sent.at[8], r6s.at[h], "gx", peer).start()
        r6[h, gx] = b6[h, gx]

    def step_pass(h):
        part = r6.at[h, pl.ds(0, G - 1)]
        with mark("w6"):
            remote(part, part, sent.at[8], r6s.at[h], "gx", gx).wait_recv()
        remote(r6.at[h], r7.at[h], sent.at[9], r7s.at[h], "ga", other).start()

    def modes_of(ref, parity):
        parts = [ref[parity * HALF + i].reshape(C * XL, Q) for i in range(HALF)]
        return jnp.concatenate(parts, axis=1)

    def gather(ref, owner, parity):
        with mark("zdot"):
            y = modes_of(ref, parity)
            for j in range(NZC):
                span = slice(j * ZC * YL, (j + 1) * ZC * YL)
                acc[:, span] = acc[:, span] + dot(y, tb[2 * owner + parity, :, span])

    def arrived(h):
        with mark("w7"):
            remote(r6.at[h], r7.at[h], sent.at[9], r7s.at[h], "ga", other).wait_recv()

    for h in range(KZ):
        step_x(h)
    for h in range(KZ - 1):
        step_y(h)
    step_mix(0)
    step_y(KZ - 1)
    for h in range(1, KZ):
        step_mix(h)
    for h in range(KZ - 1):
        step_back(h)
    step_pass(0)
    step_back(KZ - 1)
    for h in range(1, HALF):
        step_pass(h)
    gather(r6, 0, 0)
    for h in range(HALF, KZ):
        step_pass(h)
    gather(r6, 0, 1)
    for h in range(HALF):
        arrived(h)
    gather(r7, 1, 0)
    for h in range(HALF, KZ):
        arrived(h)
    with mark("final"):
        last = modes_of(r7, 1)
        for j in range(NZC):
            span = slice(j * ZC * YL, (j + 1) * ZC * YL)
            done = gelu(acc[:, span] + dot(last, tb[3, :, span])).astype(bf16)
            for z in range(ZC):
                out[j * ZC + z] = done[:, z * YL : (z + 1) * YL].reshape(C, XL, YL)

    two = state.at[pl.ds(0, STEPS), :, pl.ds(0, 2)]
    for n, (axis, ref) in enumerate(
        (
            ("gy", ys),
            ("gx", xs),
            ("ga", two),
            ("ga", lift),
            ("gx", p2.at[:, pl.ds(0, G - 1)]),
            ("gy", q3.at[:, pl.ds(0, H - 1)]),
            ("gx", r4.at[:, pl.ds(0, G - 1)]),
            ("gy", r5.at[:, pl.ds(0, H - 1)]),
            ("gx", b6.at[:, pl.ds(0, G - 1)]),
            ("ga", r6),
        )
    ):
        remote(ref, ref, sent.at[n], sent.at[n], axis, lax.axis_index(axis)).wait_send()


def east_tables(G, H, XL, C):
    CB, KB, OB = C // G, MX // H, C // G
    length = G * XL
    k = np.arange(MX) - MX // 2
    ang = 2.0 * np.pi * ((k[:, None] * np.arange(length)[None, :]) % length) / length
    scale = 1.0 / math.sqrt(length)
    cos, sin = np.cos(ang) * scale, np.sin(ang) * scale
    cos[np.abs(cos) < 1e-12] = 0.0
    sin[np.abs(sin) < 1e-12] = 0.0

    def forward(t):
        t = t.reshape(H, KB, G, XL)
        full = np.einsum("hkgx,cd->hckgdx", t, np.eye(CB))
        return full.reshape(H * CB * KB, G * CB * XL)

    def inverse(t):
        t = t.reshape(H, KB, G, XL)
        full = np.einsum("hkgx,op->goxhkp", t, np.eye(OB))
        return full.reshape(G * OB * XL, H * KB * OB)

    x1 = np.concatenate([forward(cos), forward(sin)], axis=0)
    x2 = np.concatenate([inverse(cos), -inverse(sin)], axis=0)
    return jnp.asarray(x1, bf16), jnp.asarray(x2, bf16)


def north_tables(H, YL, NZ):
    length = H * YL
    n = np.arange(MY) - MY // 2
    u = 2.0 * np.pi * ((np.arange(length)[:, None] * n[None, :]) % length) / length
    scale = 1.0 / math.sqrt(length * NZ)
    cu, su = np.cos(u) * scale, np.sin(u) * scale
    both = np.stack([np.concatenate([cu, -su], axis=1), np.concatenate([-su, -cu], axis=1)])
    both = both.reshape(2, H, YL, 2 * MY)
    return jnp.asarray(both.transpose(1, 0, 2, 3), f32), jnp.asarray(both.transpose(1, 0, 3, 2), f32)


def shards(fields, stiffness, lift_weight, lift_bias, mix_weight, spectral_weight, output_bias):
    G, H, A = (lax.axis_size(n) for n in ("gx", "gy", "ga"))
    _, NZL, NX, NY = fields.shape
    XL, YL = NX // 2, NY // 2
    C = lift_weight.shape[1]
    CB, KB, OB, KZ, Q = C // G, MX // H, C // G, MZ // A, 2 * MY
    NZ = NZL * A
    x1, x2 = east_tables(G, H, XL, C)
    ed, et = north_tables(H, YL, NZ)
    cfg = (G, H, A, C, CB, KB, OB, KZ, NZL, XL, YL)
    vmem_bytes = 67043328 - 2 * NZL * C * XL * YL
    hbm = pl.BlockSpec(memory_space=pltpu.HBM)
    LC, HALF = LIFT_CHUNKS, KZ // 2
    dma = pltpu.SemaphoreType.DMA
    V = pltpu.VMEM
    return pl.pallas_call(
        functools.partial(layer_kernel, cfg),
        out_shape=V((NZL, C, XL, YL), bf16),
        in_specs=[hbm] * 11,
        out_specs=pl.BlockSpec(memory_space=V),
        scratch_shapes=[
            V((STEPS + 1, 5, NZL + 2, NX, NY), f32),
            V((NZL, NX, NY), f32),
            V((STEPS, 2, 5, NZL, NY), bf16),
            V((STEPS, 2, 5, NZL, NY), bf16),
            V((STEPS, 2, 5, NZL * NX), f32),
            V((STEPS, 2, 5, NZL * NX), f32),
            V((5, NZL * NX, YL), f32),
            V((5, NZL, XL, YL), f32),
            V(ed.shape[1:], f32),
            V(et.shape[1:], f32),
            V(x1.shape, bf16),
            V(x2.shape, bf16),
            V(spectral_weight.shape, f32),
            V(lift_weight.shape, f32),
            V((1, C), f32),
            V(mix_weight.shape, bf16),
            V((1, C), f32),
            V((6, C * XL, YL), f32),
            V((C * XL, NZL * YL), bf16),
            V((C * XL, NZL * YL), bf16),
            V((2, C * XL, NZL * YL), bf16),
            V((2, NZL * YL, HALF * Q), bf16),
            V((2 * A, HALF * Q, NZL * YL), bf16),
            V((KZ, G, CB * XL, Q), bf16),
            V((KZ, G, CB * XL, Q), bf16),
            V((KZ, H, CB * KB, Q), bf16),
            V((KZ, H - 1, CB * KB, Q), bf16),
            V((KZ, CB * KB, Q), bf16),
            V((KZ, G, CB * KB, Q), bf16),
            V((KZ, C * KB, Q), f32),
            V((KZ, C * KB, Q), f32),
            V((KZ, KB, OB, Q), f32),
            V((KZ, H, KB * OB, Q), bf16),
            V((KZ, G, OB * XL, Q), bf16),
            V((KZ, G, OB * XL, Q), bf16),
            V((KZ, G, OB * XL, Q), bf16),
            V((C * XL, NZL * YL), f32),
            dma((11,)), dma((10,)), dma((STEPS, 3)),
            dma((LC,)), dma((KZ,)), dma((KZ,)), dma((KZ,)), dma((KZ,)), dma((KZ,)), dma((KZ,)),
        ],
        compiler_params=pltpu.CompilerParams(collective_id=0, has_side_effects=True, vmem_limit_bytes=vmem_bytes),
    )(
        fields, stiffness, ed, et, x1, x2, spectral_weight,
        lift_weight, lift_bias[None, :], mix_weight, output_bias[None, :],
    )


def solution(mesh):
    placed = (
        P(None, "ga", "gx", "gy"),
        P("ga", "gx", "gy"),
        P(),
        P(),
        P(),
        P("ga", "gy", None, "gx", None),
        P(),
    )
    return jax.shard_map(
        shards, mesh=mesh, in_specs=placed, out_specs=P("ga", None, "gx", "gy"), check_vma=False
    )
```

profile of v0, /device:TPU:0, one launch (start us, length us, event | category | flops | bytes accessed | tf_op | source)
XLA Modules:
  0.0 48.2 jit_solution(8113909143730671293)
XLA Ops:
  0.0 47.4 %shard_map.109 = bf16[8,32,8,128]{3,2,1,0:T(8,128)(2,1)S(1)} custom-call(f32[5,8,16,256]{3,2,1,0:T(8,128)} %fields_hbm.1, f32[8,16,256]{2,1,0:T(8,128)} %stiff_hbm.1, f32[4,2,128,128]{3,2,1,0:T(8,128)} %constant.10.clone.ed_hbm, f32[4,2,128,128]{3,2,1,0:T(8,128)} %constant.11.clone.et_hbm, bf16[512,256]{1,0:T(8,128)(2,1)} %constant.8.clone.x1_hbm, ...), custom_call_target="tpu_custom_call" | custom-call | tf_op jit(solution)/shard_map/pallas_call | solution.py:512
  47.4 0.8 %copy.13 = bf16[8,32,8,128]{3,2,1,0:T(8,128)(2,1)} copy(bf16[8,32,8,128]{3,2,1,0:T(8,128)(2,1)S(1)} %shard_map.109) | data formatting | bytes 1048576
where the time goes:
time: 48.7 us; the launch traced here: 48.2 us
  Pallas kernels  47.4 us (97%)
  local copies, waits for them, and re-layouts  0.8 us (2%)
    pallas_call x1, Pallas kernels, shards(): pl.pallas_call(functools.partial(layer_kernel, cfg), out_shape=V((NZL, C,...  47.4 us

commit v1 on v0

--- a/solution.py
+++ b/solution.py
@@ -15,7 +15,6 @@
 MY = 64
 MZ = 8
 DEPTH_CHUNKS = 4
-LIFT_CHUNKS = 4
 
 
 courant_half = 0.1
@@ -30,7 +29,9 @@
 
 
 def gelu(v):
-    return 0.5 * v * (1.0 + jnp.tanh(math.sqrt(2.0 / math.pi) * (v + 0.044715 * (v * v * v))))
+    scale = math.sqrt(2.0 / math.pi)
+    half = 0.5 * v
+    return half + half * jnp.tanh(v * (scale + (0.044715 * scale) * (v * v)))
 
 
 def mark(name):
@@ -116,7 +117,7 @@
     fields_hbm, stiff_hbm, ed_hbm, et_hbm, x1_hbm, x2_hbm, w_hbm, lw_hbm, lb_hbm, mix_hbm, bias_hbm,
     out,
     state, stiff, xs, xr, ys, yr, pairs, filt, ed, et, x1, x2, wv, lw, lb, mix, bias_row, wide_lift,
-    lift, lift_in, both, tf, tb, p2, r2, q3, r3, c4, r4, rr, ii, mf, r5, b6, r6, r7, acc,
+    spread_in, lift, lift_in, both, tf, tb, p2, r2, q3, r3, c4, r4, rr, ii, mf, r5, b6, r6, r7, acc,
     local, sent, hr, r1s, r2s, r3s, r4s, r5s, r6s, r7s,
 ):
     G, H, A, C, CB, KB, OB, KZ, NZL, XL, YL = cfg
@@ -135,7 +136,7 @@
         pltpu.make_async_copy(source, target, local.at[n])
         for n, (source, target) in enumerate(
             (
-                (fields_hbm, state.at[0, :, pl.ds(1, NZL)]),
+                *((fields_hbm.at[f], state.at[0, f, pl.ds(1, NZL)]) for f in range(5)),
                 (stiff_hbm, stiff),
                 (ed_hbm.at[gy], ed),
                 (et_hbm.at[gy], et),
@@ -149,7 +150,9 @@
             )
         )
     ]
-    loads[0].start()
+    first, loads = loads[:5], loads[5:]
+    for load in first:
+        load.start()
 
     HALF = KZ // 2
     NZC = DEPTH_CHUNKS
@@ -170,8 +173,8 @@
         return own([math.cos(x) for x in v]), own([math.sin(x) for x in v])
 
     def build_table():
+        loads[1].wait()
         loads[2].wait()
-        loads[3].wait()
         for z in range(NZL):
             for owner in range(A):
                 for j, k in enumerate(slots):
@@ -179,7 +182,8 @@
                     span = slice((j % HALF) * Q, (j % HALF + 1) * Q)
                     if owner == 0:
                         block = ed[0] * cos + ed[1] * sin
-                        tf[j // HALF, z * YL : (z + 1) * YL, span] = block.astype(bf16)
+                        rows = slice(z % ZC * YL, (z % ZC + 1) * YL)
+                        tf[j // HALF, z // ZC, rows, span] = block.astype(bf16)
                     block = et[0] * cos + et[1] * sin
                     tb[2 * owner + j // HALF, span, z * YL : (z + 1) * YL] = block.astype(bf16)
 
@@ -194,14 +198,28 @@
         return jnp.sum(spread * values, axis=1, keepdims=True)
 
     def build_lift():
-        for n in (7, 8):
+        for n in (6, 7):
             loads[n].wait()
+        row = lax.broadcasted_iota(jnp.int32, (C * XL, 16 * XL), 0)
+        lane = lax.broadcasted_iota(jnp.int32, (C * XL, 16 * XL), 1)
+        group = lane // XL
+        table = jnp.zeros((C * XL, 16 * XL), f32)
         for f in range(6):
-            values = lw[f : f + 1, :] if f < 5 else lb[...]
-            wide_lift[f] = jnp.broadcast_to(tall(values), (C * XL, YL))
+            values = tall(lw[f : f + 1, :] if f < 5 else lb[...])
+            high = values.astype(bf16).astype(f32)
+            rest = values - high
+            if f < 5:
+                table = jnp.where((group == f) | (group == 5 + f), high, table)
+                table = jnp.where(group == 10 + f, rest, table)
+        same = lax.rem(row, XL) == lax.rem(lane, XL)
+        table = jnp.where(same & (group < 15), table, 0.0)
+        table = jnp.where(lane == 15 * XL, high, table)
+        table = jnp.where(lane == 15 * XL + 1, rest, table)
+        wide_lift[...] = table.astype(bf16)
 
     with mark("ld0"):
-        loads[0].wait()
+        for load in first:
+            load.wait()
     eye = lax.broadcasted_iota(jnp.int32, (NZL * NX, NZL * NX), 0) == lax.broadcasted_iota(
         jnp.int32, (NZL * NX, NZL * NX), 1
     )
@@ -233,11 +251,11 @@
             remote(xs.at[t, side], xr.at[t, side], sent.at[1], hr.at[t, 1], "gx", tx).start()
             remote(now.at[:, plane], now.at[:, halo], sent.at[2], hr.at[t, 2], "ga", ta).start()
         if t == 0:
-            for load in loads[1:]:
+            for load in loads:
                 load.start()
             with mark("table"):
                 build_table()
-                loads[1].wait()
+                loads[0].wait()
         if t == STEPS - 1:
             with mark("buildlift"):
                 build_lift()
@@ -250,65 +268,59 @@
             stencil_step(now, state.at[t + 1], stiff, xr.at[t], yr.at[t], (NZL, NX, NY))
 
     with mark("filter"):
-        twin = lax.broadcasted_iota(jnp.int32, (NY, YL), 0) // 2 == lax.broadcasted_iota(
-            jnp.int32, (NY, YL), 1
-        )
-        twin = jnp.where(twin, 1.0, 0.0)
+        twin = lax.rem(lax.broadcasted_iota(jnp.int32, (2 * NY, YL), 0), NY) // 2
+        twin = jnp.where(twin == lax.broadcasted_iota(jnp.int32, (2 * NY, YL), 1), 0.25, 0.0)
         for f in range(5):
-            pairs[f] = lax.dot_general(
-                state[STEPS, f, 1 : NZL + 1].reshape(NZL * NX, NY),
-                twin,
-                (((1,), (0,)), ((), ())),
-                precision=highest,
-                preferred_element_type=f32,
-            )
-            for z in range(NZL):
-                filt[f, z] = 0.25 * (
-                    pairs[f, pl.ds(z * NX, XL, stride=2), :]
-                    + pairs[f, pl.ds(z * NX + 1, XL, stride=2), :]
-                )
-
-    def lift_two(pair, carry):
-        rows = pl.ds(pl.multiple_of(pair * 2 * XL, 2 * XL), 2 * XL)
-        weights = [wide_lift[f, rows, :] for f in range(6)]
+            v = state[STEPS, f, 1 : NZL + 1].reshape(NZL * NX, NY)
+            high = v.astype(bf16)
+            rows = pl.ds(f * NZL * NX, NZL * NX)
+            pairs[rows, :NY] = high
+            pairs[rows, NY:] = (v - high.astype(f32)).astype(bf16)
+        for rows in (pl.ds(0, 5 * NZL * XL), pl.ds(5 * NZL * XL, 5 * NZL * XL)):
+            filt[rows] = dot(pairs[rows], twin.astype(bf16))
+
+        def mean(f, z):
+            start = (f * NZL + z) * NX
+            return filt[pl.ds(start, XL, stride=2), :] + filt[pl.ds(start + 1, XL, stride=2), :]
+
         for z in range(NZL):
-            v = weights[5]
-            for f in range(5):
-                v = v + jnp.concatenate([filt[f, z], filt[f, z]], axis=0) * weights[f]
-            lift[rows, z * YL : (z + 1) * YL] = gelu(v).astype(bf16)
-        return carry
-
-    LC = LIFT_CHUNKS
-    RC = C * XL // LC
+            v = jnp.concatenate([mean(f, z) for f in range(5)], axis=0)
+            high = v.astype(bf16).astype(f32)
+            v = jnp.concatenate([high, v - high, high, jnp.ones((XL, YL), f32)], axis=0)
+            span = slice(z % ZC * YL, (z % ZC + 1) * YL)
+            spread_in[z // ZC, :, span] = v.astype(bf16)
+
     with mark("lift"):
-        for n in range(LC):
-            lax.fori_loop(n * C // 2 // LC, (n + 1) * C // 2 // LC, lift_two, 0)
-            rows = pl.ds(n * RC, RC)
-            remote(lift.at[rows], lift_in.at[rows], sent.at[3], r1s.at[n], "ga", other).start()
-    for n in range(LC):
-        rows = pl.ds(n * RC, RC)
+        for n in range(0, NZC, 2):
+            for i in range(n, n + 2):
+                lift[i] = gelu(dot(wide_lift[...], spread_in[i])).astype(bf16)
+            for i in range(n, n + 2):
+                remote(lift.at[i], lift_in.at[i], sent.at[3], r1s.at[i], "ga", other).start()
+    for n in range(NZC):
         with mark("w1"):
-            remote(lift.at[rows], lift_in.at[rows], sent.at[3], r1s.at[n], "ga", other).wait_recv()
+            remote(lift.at[n], lift_in.at[n], sent.at[3], r1s.at[n], "ga", other).wait_recv()
         with mark("sumdiff"):
-            mine, theirs = lift[rows], lift_in[rows]
-            both[0, rows] = mine + theirs
-            both[1, rows] = mine - theirs
-
-    for parity in range(2):
-        with mark("dot1"):
-            modes = dot(both[parity], tf[parity]).astype(bf16)
+            mine, theirs = lift[n], lift_in[n]
+            both[0, n] = mine + theirs
+            both[1, n] = mine - theirs
+
+    with mark("dot1"):
+        for parity in range(2):
+            modes = dot(both[parity, 0], tf[parity, 0])
+            for n in range(1, NZC):
+                modes = modes + dot(both[parity, n], tf[parity, n])
+            modes = modes.astype(bf16)
             for i in range(HALF):
-                h = parity * HALF + i
-                p2[h] = modes[:, i * Q : (i + 1) * Q].reshape(p2.shape[1:])
-        for i in range(HALF):
-            h = parity * HALF + i
-            for _, peer, _ in gx_peers:
-                remote(p2.at[h, peer], r2.at[h, gx], sent.at[4], r2s.at[h], "gx", peer).start()
-            r2[h, gx] = p2[h, gx]
+                p2[parity * HALF + i] = modes[:, i * Q : (i + 1) * Q].reshape(p2.shape[1:])
+    for h in range(KZ):
+        for _, peer, _ in gx_peers:
+            remote(p2.at[h, peer], r2.at[h, gx], sent.at[4], r2s.at[h], "gx", peer).start()
+    for h in range(KZ):
+        r2[h, gx] = p2[h, gx]
 
     with mark("direct"):
+        loads[8].wait()
         loads[9].wait()
-        loads[10].wait()
         bias = tall(bias_row[...])
         wide = dot(spread.astype(bf16), mix[...], ((1,), (1,))).astype(bf16)
         wide = dot(wide, spread.astype(bf16), ((1,), (1,)))
@@ -318,15 +330,26 @@
         mixk = jnp.where(same, wide, 0.0).astype(bf16)
         for j in range(NZC):
             span = slice(j * ZC * YL, (j + 1) * ZC * YL)
-            acc[:, span] = dot(mixk, lift[:, span]) + bias
+            acc[:, span] = dot(mixk, lift[j]) + bias
+        loads[3].wait()
         loads[4].wait()
         loads[5].wait()
-        loads[6].wait()
 
     def turn(x, v):
-        both_parts = dot(x[...], v)
-        rows = both_parts.shape[0] // 2
-        return (both_parts[:rows] + swapped(both_parts[rows:])).astype(bf16)
+        rows = x.shape[0] // 2
+        return (dot(x[:rows], v) + swapped(dot(x[rows:], v))).astype(bf16)
+
+    def staggered(h, send):
+        @pl.when(ga == 0)
+        def _():
+            send(h)
+
+        if h == KZ - 1:
+
+            @pl.when(ga != 0)
+            def _():
+                for i in range(KZ):
+                    send(i)
 
     def step_x(h):
         part = r2.at[h, pl.ds(0, G - 1)]
@@ -334,6 +357,9 @@
             remote(part, part, sent.at[4], r2s.at[h], "gx", gx).wait_recv()
         with mark("xdot"):
             q3[h] = turn(x1, r2[h].reshape(C * XL, Q)).reshape(q3.shape[1:])
+        staggered(h, send_x)
+
+    def send_x(h):
         for n, peer, _ in gy_peers:
             remote(q3.at[h, peer], r3.at[h, n - 1], sent.at[5], r3s.at[h], "gy", peer).start()
 
@@ -348,33 +374,39 @@
             remote(c4.at[h], r4.at[h, gx], sent.at[6], r4s.at[h], "gx", peer).start()
         r4[h, gx] = c4[h]
 
-    low = lax.broadcasted_iota(jnp.int32, (C * KB, Q), 1) < MY
+    low = lax.broadcasted_iota(jnp.int32, (CB * KB, Q), 1) < MY
 
     def step_mix(h):
         part = r4.at[h, pl.ds(0, G - 1)]
         with mark("w4"):
             remote(part, part, sent.at[6], r4s.at[h], "gx", gx).wait_recv()
         with mark("mix"):
-            v = r4[h].reshape(C * KB, Q).astype(f32)
-            turned = pltpu.roll(v, MY, 1)
-            rr[h] = jnp.where(low, v, turned)
-            ii[h] = jnp.where(low, turned, v)
+            for g in range(G):
+                v = r4[h, g].astype(f32)
+                turned = pltpu.roll(v, MY, 1)
+                rows = pl.ds(g * CB, CB)
+                rr[h, :, rows, :] = jnp.where(low, v, turned).reshape(KB, CB, Q)
+                ii[h, :, rows, :] = jnp.where(low, turned, v).reshape(KB, CB, Q)
 
             def mix_one(kx, carry):
                 a = [None] * 4
                 b = [None] * 4
                 for c in range(C):
                     w = wv[slots[h], kx, c]
-                    x = w * rr[h, pl.ds(c * KB + kx, 1), :]
-                    y = w * ii[h, pl.ds(c * KB + kx, 1), :]
+                    x = w * rr[h, kx, c : c + 1, :]
+                    y = w * ii[h, kx, c : c + 1, :]
                     n = c % 4
                     a[n] = x if a[n] is None else a[n] + x
                     b[n] = y if b[n] is None else b[n] + y
                 mf[h, kx] = ((a[0] + a[1]) + (a[2] + a[3])) - swapped((b[0] + b[1]) + (b[2] + b[3]))
                 return carry
 
-            lax.fori_loop(0, KB, mix_one, 0)
+            for kx in range(KB):
+                mix_one(kx, 0)
             r5[h, gy] = mf[h].reshape(KB * OB, Q).astype(bf16)
+        staggered(h, send_mix)
+
+    def send_mix(h):
         for _, peer, _ in gy_peers:
             remote(r5.at[h, gy], r5.at[h, gy], sent.at[7], r5s.at[h], "gy", peer).start()
 
@@ -411,17 +443,13 @@
 
     for h in range(KZ):
         step_x(h)
-    for h in range(KZ - 1):
+    for h in range(KZ):
         step_y(h)
-    step_mix(0)
-    step_y(KZ - 1)
-    for h in range(1, KZ):
+    for h in range(KZ):
         step_mix(h)
-    for h in range(KZ - 1):
+    for h in range(KZ):
         step_back(h)
-    step_pass(0)
-    step_back(KZ - 1)
-    for h in range(1, HALF):
+    for h in range(HALF):
         step_pass(h)
     gather(r6, 0, 0)
     for h in range(HALF, KZ):
@@ -470,7 +498,7 @@
 
     def forward(t):
         t = t.reshape(H, KB, G, XL)
-        full = np.einsum("hkgx,cd->hckgdx", t, np.eye(CB))
+        full = np.einsum("hkgx,cd->hkcgdx", t, np.eye(CB))
         return full.reshape(H * CB * KB, G * CB * XL)
 
     def inverse(t):
@@ -506,7 +534,8 @@
     cfg = (G, H, A, C, CB, KB, OB, KZ, NZL, XL, YL)
     vmem_bytes = 67043328 - 2 * NZL * C * XL * YL
     hbm = pl.BlockSpec(memory_space=pltpu.HBM)
-    LC, HALF = LIFT_CHUNKS, KZ // 2
+    NZC, HALF = DEPTH_CHUNKS, KZ // 2
+    ZW = NZL // NZC * YL
     dma = pltpu.SemaphoreType.DMA
     V = pltpu.VMEM
     return pl.pallas_call(
@@ -521,8 +550,8 @@
             V((STEPS, 2, 5, NZL, NY), bf16),
             V((STEPS, 2, 5, NZL * NX), f32),
             V((STEPS, 2, 5, NZL * NX), f32),
-            V((5, NZL * NX, YL), f32),
-            V((5, NZL, XL, YL), f32),
+            V((5 * NZL * NX, 2 * NY), bf16),
+            V((5 * NZL * NX, YL), f32),
             V(ed.shape[1:], f32),
             V(et.shape[1:], f32),
             V(x1.shape, bf16),
@@ -532,11 +561,12 @@
             V((1, C), f32),
             V(mix_weight.shape, bf16),
             V((1, C), f32),
-            V((6, C * XL, YL), f32),
-            V((C * XL, NZL * YL), bf16),
-            V((C * XL, NZL * YL), bf16),
-            V((2, C * XL, NZL * YL), bf16),
-            V((2, NZL * YL, HALF * Q), bf16),
+            V((C * XL, 16 * XL), bf16),
+            V((NZC, 16 * XL, ZW), bf16),
+            V((NZC, C * XL, ZW), bf16),
+            V((NZC, C * XL, ZW), bf16),
+            V((2, NZC, C * XL, ZW), bf16),
+            V((2, NZC, ZW, HALF * Q), bf16),
             V((2 * A, HALF * Q, NZL * YL), bf16),
             V((KZ, G, CB * XL, Q), bf16),
             V((KZ, G, CB * XL, Q), bf16),
@@ -544,16 +574,16 @@
             V((KZ, H - 1, CB * KB, Q), bf16),
             V((KZ, CB * KB, Q), bf16),
             V((KZ, G, CB * KB, Q), bf16),
-            V((KZ, C * KB, Q), f32),
-            V((KZ, C * KB, Q), f32),
+            V((KZ, KB, C, Q), f32),
+            V((KZ, KB, C, Q), f32),
             V((KZ, KB, OB, Q), f32),
             V((KZ, H, KB * OB, Q), bf16),
             V((KZ, G, OB * XL, Q), bf16),
             V((KZ, G, OB * XL, Q), bf16),
             V((KZ, G, OB * XL, Q), bf16),
             V((C * XL, NZL * YL), f32),
-            dma((11,)), dma((10,)), dma((STEPS, 3)),
-            dma((LC,)), dma((KZ,)), dma((KZ,)), dma((KZ,)), dma((KZ,)), dma((KZ,)), dma((KZ,)),
+            dma((15,)), dma((10,)), dma((STEPS, 3)),
+            dma((NZC,)), dma((KZ,)), dma((KZ,)), dma((KZ,)), dma((KZ,)), dma((KZ,)), dma((KZ,)),
         ],
         compiler_params=pltpu.CompilerParams(collective_id=0, has_side_effects=True, vmem_limit_bytes=vmem_bytes),
     )(

time: 48.7 us -> 45.8 us (0.940)
  Pallas kernels: 47.4 us -> 44.8 us
    pallas_call x1, Pallas kernels: 47.4 us -> 44.8 us  [shards(): pl.pallas_call(functools.partial(layer_kernel, cfg), out_shape=V((NZL, C,...]
where the time goes in v1:
time: 45.8 us; the launch traced here: 45.6 us
  Pallas kernels  44.8 us (98%)
  local copies, waits for them, and re-layouts  0.8 us (2%)
    pallas_call x1, Pallas kernels, shards(): pl.pallas_call(functools.partial(layer_kernel, cfg), out_shape=V((NZL, C,...  44.8 us

profile of v1, /device:TPU:0, one launch (start us, length us, event | category | flops | bytes accessed | tf_op | source)
XLA Modules:
  0.0 45.6 jit_solution(11796197963107202686)
XLA Ops:
  0.0 44.8 %shard_map.109 = bf16[8,32,8,128]{3,2,1,0:T(8,128)(2,1)S(1)} custom-call(f32[5,8,16,256]{3,2,1,0:T(8,128)} %fields_hbm.1, f32[8,16,256]{2,1,0:T(8,128)} %stiff_hbm.1, f32[4,2,128,128]{3,2,1,0:T(8,128)} %constant.10.clone.ed_hbm, f32[4,2,128,128]{3,2,1,0:T(8,128)} %constant.11.clone.et_hbm, bf16[512,256]{1,0:T(8,128)(2,1)} %constant.8.clone.x1_hbm, ...), custom_call_target="tpu_custom_call" | custom-call | tf_op jit(solution)/shard_map/pallas_call | solution.py:541
  44.9 0.8 %copy.13 = bf16[8,32,8,128]{3,2,1,0:T(8,128)(2,1)} copy(bf16[8,32,8,128]{3,2,1,0:T(8,128)(2,1)S(1)} %shard_map.109) | data formatting | bytes 1048576

commit v2 on v1

--- a/solution.py
+++ b/solution.py
@@ -47,10 +47,25 @@
     return lax.dot_general(a, b, (dims, ((), ())), preferred_element_type=f32)
 
 
-def peers(axis):
+def line_peers(axis):
     count = lax.axis_size(axis)
     me = lax.axis_index(axis)
-    return me, [(d, lax.rem(me + d, count), lax.rem(me + count - d, count)) for d in range(1, count)]
+    order = []
+    for j in range(count - 1):
+        down, up = count - 1 - j, j
+        down = jnp.where(down <= me, down - 1, down)
+        up = jnp.where(up >= me, up + 1, up)
+        order.append(jnp.where(me < count // 2, down, up))
+    return me, order
+
+
+def square_peers(axis):
+    count = lax.axis_size(axis)
+    me = lax.axis_index(axis)
+    if count != 4:
+        return line_peers(axis)
+    flip_x = me + 1 - 2 * lax.rem(me, 2)
+    return me, [3 - me, 3 - flip_x, flip_x]
 
 
 def remote(src, dst, send, recv, axis, peer):
@@ -80,18 +95,20 @@
         ]
         for side in range(2)
     ]
-    row = lax.broadcasted_iota(jnp.int32, (NX, NY), 0)
-    lane = lax.broadcasted_iota(jnp.int32, (NX, NY), 1)
-    a, b = courant_half, smooth_half
+    weights = [
+        ((smooth_half + courant_half * flow) / courant_half, (smooth_half - courant_half * flow) / courant_half)
+        for flow in mean_flow
+    ]
+    keep = (1.0 - 6.0 * smooth_half) / courant_half
     for z in range(NZ):
         near = []
         for f in range(5):
             c = state[f, z + 1]
             span = slice(z * NX, (z + 1) * NX)
-            xl = jnp.where(row == 0, xr[0, f, z : z + 1, :].astype(f32), pltpu.roll(c, 1, 0))
-            xu = jnp.where(row == NX - 1, xr[1, f, z : z + 1, :].astype(f32), pltpu.roll(c, NX - 1, 0))
-            yl = jnp.where(lane == 0, columns[0][f][span], pltpu.roll(c, 1, 1))
-            yu = jnp.where(lane == NY - 1, columns[1][f][span], pltpu.roll(c, NY - 1, 1))
+            xl = shifted(c, xr[0, f, z : z + 1, :].astype(f32), 0, 1, 8)
+            xu = shifted(c, xr[1, f, z : z + 1, :].astype(f32), 0, -1, 8)
+            yl = shifted(c, columns[0][f][span], 1, 1, 128)
+            yu = shifted(c, columns[1][f][span], 1, -1, 128)
             near.append((c, xl, xu, yl, yu, state[f, z], state[f, z + 2]))
         diverge = (
             (near[1][2] - near[1][1]) + (near[2][4] - near[2][3]) + (near[3][6] - near[3][5])
@@ -100,16 +117,20 @@
         coupling = (diverge, p[2] - p[1], p[4] - p[3], p[6] - p[5], stiff[z] * diverge)
         for f in range(5):
             c, xl, xu, yl, yu, zl, zu = near[f]
-            target[f, z + 1] = (
-                (1.0 - 6.0 * b) * c
-                + (b + a * mean_flow[0]) * xl
-                + (b - a * mean_flow[0]) * xu
-                + (b + a * mean_flow[1]) * yl
-                + (b - a * mean_flow[1]) * yu
-                + (b + a * mean_flow[2]) * zl
-                + (b - a * mean_flow[2]) * zu
-                - a * coupling[f]
-            )
+            total = c if abs(keep - 1.0) < 1e-12 else keep * c
+            for (low, high), lower, upper in zip(weights, (xl, yl, zl), (xu, yu, zu)):
+                total = total + (low * lower + high * upper)
+            target[f, z + 1] = total - coupling[f]
+
+
+def shifted(c, halo, axis, step, tile):
+    count = c.shape[axis] // tile
+    pieces = [lax.slice_in_dim(c, i * tile, (i + 1) * tile, axis=axis) for i in range(count)]
+    rolled = [pltpu.roll(piece, step % tile, axis) for piece in pieces]
+    edge = 0 if step > 0 else tile - 1
+    at_edge = lax.broadcasted_iota(jnp.int32, pieces[0].shape, axis) == edge
+    before = [halo] + rolled[:-1] if step > 0 else rolled[1:] + [halo]
+    return jnp.concatenate([jnp.where(at_edge, b, r) for b, r in zip(before, rolled)], axis=axis)
 
 
 def layer_kernel(
@@ -123,20 +144,20 @@
     G, H, A, C, CB, KB, OB, KZ, NZL, XL, YL = cfg
     Q = 2 * MY
     NX, NY = 2 * XL, 2 * YL
-    gx, gx_peers = peers("gx")
-    gy, gy_peers = peers("gy")
+    gx, gx_peers = square_peers("gx")
+    gy, gy_peers = line_peers("gy")
     ga = lax.axis_index("ga")
     other = lax.rem(ga + 1, A)
     barrier = pltpu.get_barrier_semaphore()
     for axis, group in (("gx", gx_peers), ("gy", gy_peers)):
-        for _, peer, _ in group:
+        for peer in group:
             pl.semaphore_signal(barrier, inc=1, device_id={axis: peer}, device_id_type=MESH)
     pl.semaphore_signal(barrier, inc=1, device_id={"ga": other}, device_id_type=MESH)
     loads = [
         pltpu.make_async_copy(source, target, local.at[n])
         for n, (source, target) in enumerate(
             (
-                *((fields_hbm.at[f], state.at[0, f, pl.ds(1, NZL)]) for f in range(5)),
+                (fields_hbm, state.at[0, :, pl.ds(1, NZL)]),
                 (stiff_hbm, stiff),
                 (ed_hbm.at[gy], ed),
                 (et_hbm.at[gy], et),
@@ -150,9 +171,8 @@
             )
         )
     ]
-    first, loads = loads[:5], loads[5:]
-    for load in first:
-        load.start()
+    first, loads = loads[0], loads[1:]
+    first.start()
 
     HALF = KZ // 2
     NZC = DEPTH_CHUNKS
@@ -218,8 +238,7 @@
         wide_lift[...] = table.astype(bf16)
 
     with mark("ld0"):
-        for load in first:
-            load.wait()
+        first.wait()
     eye = lax.broadcasted_iota(jnp.int32, (NZL * NX, NZL * NX), 0) == lax.broadcasted_iota(
         jnp.int32, (NZL * NX, NZL * NX), 1
     )
@@ -241,15 +260,14 @@
             with mark("barrier"):
                 pl.semaphore_wait(barrier, (G - 1) + (H - 1) + 1)
         for side in range(2):
-            shift = 1 if side == 0 else -1
-            tx, ty, ta = (
-                lax.rem(lax.axis_index(n) + lax.axis_size(n) + shift, lax.axis_size(n))
-                for n in ("gx", "gy", "ga")
-            )
-            plane, halo = (NZL, 0) if side == 0 else (1, NZL + 1)
+            ty = lax.rem(gy + H + (1 if side == 0 else -1), H)
             remote(ys.at[t, side], yr.at[t, side], sent.at[0], hr.at[t, 0], "gy", ty).start()
+        for turn_of in range(2):
+            side = lax.rem(gx + 1 + turn_of, 2)
+            tx = lax.rem(gx + G + 1 - 2 * side, G)
             remote(xs.at[t, side], xr.at[t, side], sent.at[1], hr.at[t, 1], "gx", tx).start()
-            remote(now.at[:, plane], now.at[:, halo], sent.at[2], hr.at[t, 2], "ga", ta).start()
+        for plane, halo in ((NZL, 0), (1, NZL + 1)):
+            remote(now.at[:, plane], now.at[:, halo], sent.at[2], hr.at[t, 2], "ga", other).start()
         if t == 0:
             for load in loads:
                 load.start()
@@ -269,7 +287,7 @@
 
     with mark("filter"):
         twin = lax.rem(lax.broadcasted_iota(jnp.int32, (2 * NY, YL), 0), NY) // 2
-        twin = jnp.where(twin == lax.broadcasted_iota(jnp.int32, (2 * NY, YL), 1), 0.25, 0.0)
+        twin = jnp.where(twin == lax.broadcasted_iota(jnp.int32, (2 * NY, YL), 1), 1.0, 0.0)
         for f in range(5):
             v = state[STEPS, f, 1 : NZL + 1].reshape(NZL * NX, NY)
             high = v.astype(bf16)
@@ -281,7 +299,8 @@
 
         def mean(f, z):
             start = (f * NZL + z) * NX
-            return filt[pl.ds(start, XL, stride=2), :] + filt[pl.ds(start + 1, XL, stride=2), :]
+            both_rows = filt[pl.ds(start, XL, stride=2), :] + filt[pl.ds(start + 1, XL, stride=2), :]
+            return both_rows * (0.25 * courant_half**STEPS)
 
         for z in range(NZL):
             v = jnp.concatenate([mean(f, z) for f in range(5)], axis=0)
@@ -313,7 +332,7 @@
             for i in range(HALF):
                 p2[parity * HALF + i] = modes[:, i * Q : (i + 1) * Q].reshape(p2.shape[1:])
     for h in range(KZ):
-        for _, peer, _ in gx_peers:
+        for peer in gx_peers:
             remote(p2.at[h, peer], r2.at[h, gx], sent.at[4], r2s.at[h], "gx", peer).start()
     for h in range(KZ):
         r2[h, gx] = p2[h, gx]
@@ -339,16 +358,16 @@
         rows = x.shape[0] // 2
         return (dot(x[:rows], v) + swapped(dot(x[rows:], v))).astype(bf16)
 
-    def staggered(h, send):
+    def staggered(h, send, size):
         @pl.when(ga == 0)
         def _():
             send(h)
 
-        if h == KZ - 1:
+        if (h + 1) % size == 0:
 
             @pl.when(ga != 0)
             def _():
-                for i in range(KZ):
+                for i in range(h + 1 - size, h + 1):
                     send(i)
 
     def step_x(h):
@@ -357,20 +376,21 @@
             remote(part, part, sent.at[4], r2s.at[h], "gx", gx).wait_recv()
         with mark("xdot"):
             q3[h] = turn(x1, r2[h].reshape(C * XL, Q)).reshape(q3.shape[1:])
-        staggered(h, send_x)
+        staggered(h, send_x, KZ)
 
     def send_x(h):
-        for n, peer, _ in gy_peers:
-            remote(q3.at[h, peer], r3.at[h, n - 1], sent.at[5], r3s.at[h], "gy", peer).start()
+        for peer in gy_peers:
+            remote(q3.at[h, peer], r3.at[h, gy], sent.at[5], r3s.at[h], "gy", peer).start()
 
     def step_y(h):
         with mark("w3"):
-            remote(r3.at[h], r3.at[h], sent.at[5], r3s.at[h], "gy", gy).wait_recv()
+            part = r3.at[h, pl.ds(0, H - 1)]
+            remote(part, part, sent.at[5], r3s.at[h], "gy", gy).wait_recv()
         total = q3[h, gy].astype(f32)
-        for n in range(H - 1):
-            total = total + r3[h, n].astype(f32)
+        for peer in gy_peers:
+            total = total + r3[h, peer].astype(f32)
         c4[h] = total.astype(bf16)
-        for _, peer, _ in gx_peers:
+        for peer in gx_peers:
             remote(c4.at[h], r4.at[h, gx], sent.at[6], r4s.at[h], "gx", peer).start()
         r4[h, gx] = c4[h]
 
@@ -404,10 +424,10 @@
             for kx in range(KB):
                 mix_one(kx, 0)
             r5[h, gy] = mf[h].reshape(KB * OB, Q).astype(bf16)
-        staggered(h, send_mix)
+        staggered(h, send_mix, HALF)
 
     def send_mix(h):
-        for _, peer, _ in gy_peers:
+        for peer in gy_peers:
             remote(r5.at[h, gy], r5.at[h, gy], sent.at[7], r5s.at[h], "gy", peer).start()
 
     def step_back(h):
@@ -416,7 +436,7 @@
             remote(part, part, sent.at[7], r5s.at[h], "gy", gy).wait_recv()
         with mark("back"):
             b6[h] = turn(x2, r5[h].reshape(H * KB * OB, Q)).reshape(b6.shape[1:])
-        for _, peer, _ in gx_peers:
+        for peer in gx_peers:
             remote(b6.at[h, peer], r6.at[h, gx], sent.at[8], r6s.at[h], "gx", peer).start()
         r6[h, gx] = b6[h, gx]
 
@@ -571,7 +591,7 @@
             V((KZ, G, CB * XL, Q), bf16),
             V((KZ, G, CB * XL, Q), bf16),
             V((KZ, H, CB * KB, Q), bf16),
-            V((KZ, H - 1, CB * KB, Q), bf16),
+            V((KZ, H, CB * KB, Q), bf16),
             V((KZ, CB * KB, Q), bf16),
             V((KZ, G, CB * KB, Q), bf16),
             V((KZ, KB, C, Q), f32),
@@ -582,7 +602,7 @@
             V((KZ, G, OB * XL, Q), bf16),
             V((KZ, G, OB * XL, Q), bf16),
             V((C * XL, NZL * YL), f32),
-            dma((15,)), dma((10,)), dma((STEPS, 3)),
+            dma((11,)), dma((10,)), dma((STEPS, 3)),
             dma((NZC,)), dma((KZ,)), dma((KZ,)), dma((KZ,)), dma((KZ,)), dma((KZ,)), dma((KZ,)),
         ],
         compiler_params=pltpu.CompilerParams(collective_id=0, has_side_effects=True, vmem_limit_bytes=vmem_bytes),

time: 45.8 us -> 46.6 us (1.017)
  Pallas kernels: 44.8 us -> 45.7 us
    pallas_call x1, Pallas kernels: 44.8 us -> 45.7 us  [shards(): pl.pallas_call(functools.partial(layer_kernel, cfg), out_shape=V((NZL, C,...]
where the time goes in v2:
time: 46.6 us; the launch traced here: 46.5 us
  Pallas kernels  45.7 us (98%)
  local copies, waits for them, and re-layouts  0.8 us (2%)
    pallas_call x1, Pallas kernels, shards(): pl.pallas_call(functools.partial(layer_kernel, cfg), out_shape=V((NZL, C,...  45.7 us

profile of v2, /device:TPU:0, one launch (start us, length us, event | category | flops | bytes accessed | tf_op | source)
XLA Modules:
  0.0 46.5 jit_solution(12627477196996253797)
XLA Ops:
  0.0 45.7 %shard_map.109 = bf16[8,32,8,128]{3,2,1,0:T(8,128)(2,1)S(1)} custom-call(f32[5,8,16,256]{3,2,1,0:T(8,128)} %fields_hbm.1, f32[8,16,256]{2,1,0:T(8,128)} %stiff_hbm.1, f32[4,2,128,128]{3,2,1,0:T(8,128)} %constant.10.clone.ed_hbm, f32[4,2,128,128]{3,2,1,0:T(8,128)} %constant.11.clone.et_hbm, bf16[512,256]{1,0:T(8,128)(2,1)} %constant.8.clone.x1_hbm, ...), custom_call_target="tpu_custom_call" | custom-call | tf_op jit(solution)/shard_map/pallas_call | solution.py:561
  45.7 0.8 %copy.13 = bf16[8,32,8,128]{3,2,1,0:T(8,128)(2,1)} copy(bf16[8,32,8,128]{3,2,1,0:T(8,128)(2,1)S(1)} %shard_map.109) | data formatting | bytes 1048576

commit v3 on v2

--- a/solution.py
+++ b/solution.py
@@ -32,10 +32,6 @@
     scale = math.sqrt(2.0 / math.pi)
     half = 0.5 * v
     return half + half * jnp.tanh(v * (scale + (0.044715 * scale) * (v * v)))
-
-
-def mark(name):
-    return contextlib.nullcontext()
 
 
 def swapped(v):
@@ -139,11 +135,23 @@
     out,
     state, stiff, xs, xr, ys, yr, pairs, filt, ed, et, x1, x2, wv, lw, lb, mix, bias_row, wide_lift,
     spread_in, lift, lift_in, both, tf, tb, p2, r2, q3, r3, c4, r4, rr, ii, mf, r5, b6, r6, r7, acc,
-    local, sent, hr, r1s, r2s, r3s, r4s, r5s, r6s, r7s,
+    local, sent, hr, r1s, r2s, r3s, r4s, r5s, r6s, r7s, wall,
 ):
     G, H, A, C, CB, KB, OB, KZ, NZL, XL, YL = cfg
     Q = 2 * MY
     NX, NY = 2 * XL, 2 * YL
+
+    def fence():
+        @pl.when(lax.axis_index("ga") < 0)
+        def _():
+            wall[...] = jnp.zeros_like(wall)
+
+    @contextlib.contextmanager
+    def mark(name):
+        fence()
+        yield
+        fence()
+
     gx, gx_peers = square_peers("gx")
     gy, gy_peers = line_peers("gy")
     ga = lax.axis_index("ga")
@@ -244,24 +252,25 @@
     )
     for t in range(STEPS):
         now = state.at[t]
-        with mark("pack%d" % t):
-            for side, (edge_x, edge_y) in enumerate(((NX - 1, NY - 1), (0, 0))):
-                for f in range(5):
-                    for z in range(NZL):
-                        row = now[f, z + 1, edge_x : edge_x + 1, :]
-                        xs[t, side, f, z : z + 1, :] = row.astype(bf16)
-                    column = now[f, 1 : NZL + 1, :, edge_y : edge_y + 1].reshape(NZL * NX, 1)
-                    ys[t, side, f : f + 1, :] = jnp.sum(
-                        jnp.where(eye, jnp.broadcast_to(column, eye.shape), 0.0),
-                        axis=0,
-                        keepdims=True,
-                    )
+        for side, edge in enumerate((NY - 1, 0)):
+            for f in range(5):
+                column = now[f, 1 : NZL + 1, :, edge : edge + 1].reshape(NZL * NX, 1)
+                ys[t, side, f : f + 1, :] = jnp.sum(
+                    jnp.where(eye, jnp.broadcast_to(column, eye.shape), 0.0),
+                    axis=0,
+                    keepdims=True,
+                )
         if t == 0:
             with mark("barrier"):
                 pl.semaphore_wait(barrier, (G - 1) + (H - 1) + 1)
         for side in range(2):
             ty = lax.rem(gy + H + (1 if side == 0 else -1), H)
             remote(ys.at[t, side], yr.at[t, side], sent.at[0], hr.at[t, 0], "gy", ty).start()
+        for side, edge in enumerate((NX - 1, 0)):
+            for f in range(5):
+                for z in range(NZL):
+                    row = now[f, z + 1, edge : edge + 1, :]
+                    xs[t, side, f, z : z + 1, :] = row.astype(bf16)
         for turn_of in range(2):
             side = lax.rem(gx + 1 + turn_of, 2)
             tx = lax.rem(gx + G + 1 - 2 * side, G)
@@ -604,6 +613,7 @@
             V((C * XL, NZL * YL), f32),
             dma((11,)), dma((10,)), dma((STEPS, 3)),
             dma((NZC,)), dma((KZ,)), dma((KZ,)), dma((KZ,)), dma((KZ,)), dma((KZ,)), dma((KZ,)),
+            V((8, 128), f32),
         ],
         compiler_params=pltpu.CompilerParams(collective_id=0, has_side_effects=True, vmem_limit_bytes=vmem_bytes),
     )(

time: 46.6 us -> 45 us (0.966)
  Pallas kernels: 45.7 us -> 44.1 us
    pallas_call x1, Pallas kernels: 45.7 us -> 44.1 us  [shards(): pl.pallas_call(functools.partial(layer_kernel, cfg), out_shape=V((NZL, C,...]
where the time goes in v3:
time: 45 us; the launch traced here: 44.9 us
  Pallas kernels  44.1 us (98%)
  local copies, waits for them, and re-layouts  0.8 us (2%)
    pallas_call x1, Pallas kernels, shards(): pl.pallas_call(functools.partial(layer_kernel, cfg), out_shape=V((NZL, C,...  44.1 us

profile of v3, /device:TPU:0, one launch (start us, length us, event | category | flops | bytes accessed | tf_op | source)
XLA Modules:
  0.0 44.9 jit_solution(1080653208065847698)
XLA Ops:
  0.0 44.1 %shard_map.109 = bf16[8,32,8,128]{3,2,1,0:T(8,128)(2,1)S(1)} custom-call(f32[5,8,16,256]{3,2,1,0:T(8,128)} %fields_hbm.1, f32[8,16,256]{2,1,0:T(8,128)} %stiff_hbm.1, f32[4,2,128,128]{3,2,1,0:T(8,128)} %constant.10.clone.ed_hbm, f32[4,2,128,128]{3,2,1,0:T(8,128)} %constant.11.clone.et_hbm, bf16[512,256]{1,0:T(8,128)(2,1)} %constant.8.clone.x1_hbm, ...), custom_call_target="tpu_custom_call" | custom-call | tf_op jit(solution)/shard_map/pallas_call | solution.py:570
  44.1 0.8 %copy.13 = bf16[8,32,8,128]{3,2,1,0:T(8,128)(2,1)} copy(bf16[8,32,8,128]{3,2,1,0:T(8,128)(2,1)S(1)} %shard_map.109) | data formatting | bytes 1048576

commit v4 on v3

--- a/solution.py
+++ b/solution.py
@@ -150,7 +150,6 @@
     def mark(name):
         fence()
         yield
-        fence()
 
     gx, gx_peers = square_peers("gx")
     gy, gy_peers = line_peers("gy")

time: 45 us -> 44.9 us (level)
  no operation moved by 1% of the time
where the time goes in v4:
time: 44.9 us; the launch traced here: 44.7 us
  Pallas kernels  43.9 us (98%)
  local copies, waits for them, and re-layouts  0.8 us (2%)
    pallas_call x1, Pallas kernels, shards(): pl.pallas_call(functools.partial(layer_kernel, cfg), out_shape=V((NZL, C,...  43.9 us

profile of v4, /device:TPU:0, one launch (start us, length us, event | category | flops | bytes accessed | tf_op | source)
XLA Modules:
  0.0 44.7 jit_solution(17243975056563130253)
XLA Ops:
  0.0 43.9 %shard_map.109 = bf16[8,32,8,128]{3,2,1,0:T(8,128)(2,1)S(1)} custom-call(f32[5,8,16,256]{3,2,1,0:T(8,128)} %fields_hbm.1, f32[8,16,256]{2,1,0:T(8,128)} %stiff_hbm.1, f32[4,2,128,128]{3,2,1,0:T(8,128)} %constant.10.clone.ed_hbm, f32[4,2,128,128]{3,2,1,0:T(8,128)} %constant.11.clone.et_hbm, bf16[512,256]{1,0:T(8,128)(2,1)} %constant.8.clone.x1_hbm, ...), custom_call_target="tpu_custom_call" | custom-call | tf_op jit(solution)/shard_map/pallas_call | solution.py:569
  43.9 0.8 %copy.13 = bf16[8,32,8,128]{3,2,1,0:T(8,128)(2,1)} copy(bf16[8,32,8,128]{3,2,1,0:T(8,128)(2,1)S(1)} %shard_map.109) | data formatting | bytes 1048576
